TPU v7x, 32 devices: a whole 2x2x4 slice. The times are simulated.
32 devices in a mesh: head: 8 (over z, y), fsdp: 4 (over x, core).
Axes of the slice: x: 2, y: 2, z: 4, core: 2. Of those that a mesh axis runs over, the one named last changes fastest.
Arguments:
- hidden: bfloat16 [4, 1024, 2048], P('fsdp', 'head'), may hold values from -6 to 6
- w_qkv: bfloat16 [2048, 6144], P(('head', 'fsdp')), may hold values from -0.125 to 0.125
- w_out: bfloat16 [2048, 2048], P(('head', 'fsdp')), may hold values from -0.75 to 0.75
- w_router: bfloat16 [2048, 16], P(('head', 'fsdp')), may hold values from -0.0625 to 0.0625
- g_attn: bfloat16 [2048], P(('head', 'fsdp')), may hold values from 0.099609375 to 1.8984375
- g_ffn: bfloat16 [2048], P(('head', 'fsdp')), may hold values from 0.099609375 to 1.8984375
- g_q: bfloat16 [2048], P(('head', 'fsdp')), may hold values from 0.69921875 to 2
- g_k: bfloat16 [2048], P(('head', 'fsdp')), may hold values from 0.69921875 to 2
- w_gate: bfloat16 [16, 2048, 1024], P('head', 'fsdp'), may hold values from -0.125 to 0.125
- w_up: bfloat16 [16, 2048, 1024], P('head', 'fsdp'), may hold values from -0.125 to 0.125
- w_down: bfloat16 [16, 1024, 2048], P('head', 'fsdp'), may hold values from -0.75 to 0.75
- lengths: int32 [4], P('fsdp'), may hold values from 256 to 1024, as said below
- routes: int32 [4, 1024, 8], P('fsdp', 'head'), may hold values from 0 to 15, all different within a row; in each aligned block of 128 rows (0 to 127, 128 to 255, ..., all dimensions but the last counted through in order) at most 96 rows name the same one
- route_codes: int32 [4, 1024, 8], P('fsdp', 'head'), may hold values from -384 to 383
- cotangent: bfloat16 [4, 1024, 2048], P('fsdp', 'head'), may hold values from -6 to 6
Outputs:
- out: bfloat16 [4, 1024, 2048], P('fsdp', 'head')
- d_hidden: float32 [4, 1024, 2048], P('fsdp', 'head')
- d_w_qkv: float32 [2048, 6144], P(('head', 'fsdp'))
- d_w_out: float32 [2048, 2048], P(('head', 'fsdp'))
- d_w_router: float32 [2048, 16], P(('head', 'fsdp'))
- d_g_attn: float32 [2048], P(('head', 'fsdp'))
- d_g_ffn: float32 [2048], P(('head', 'fsdp'))
- d_g_q: float32 [2048], P(('head', 'fsdp'))
- d_g_k: float32 [2048], P(('head', 'fsdp'))
- d_w_gate: float32 [16, 2048, 1024], P('head', 'fsdp')
- d_w_up: float32 [16, 2048, 1024], P('head', 'fsdp')
- d_w_down: float32 [16, 1024, 2048], P('head', 'fsdp')
Inputs may be any that keep to these rules, and one draw needn't show every extreme that they name: `lengths`: keys at positions at or after a sequence's length are masked. Some sequence has 1024 valid slots, some 1024 // 4. Each token names 8 different experts. In the 128 tokens of one device no expert is named by more than 96 routes, and some expert reaches 96.
All inputs are finite; a program needn't handle non-finite values.
Results may differ from a plain program's by a relative error of at most 0.018.
Values may be sent and summed in bfloat16 or wider, within the bound.
A program may use at most 256 MiB of HBM per device.

v0:
```python
import math
import jax
import jax.numpy as jnp
from jax import lax
from jax.sharding import PartitionSpec as P

HEADS = 16
HD = 128
FF = 1024
TOP = 8
EXP_DEV = 2
EPS = 1e-06
ROPE_BASE = 10000.0
NEGATIVE = -1e30
BF = jnp.bfloat16
F32 = jnp.float32


def ring_head(n, k):
    k %= n
    return 2 * k if k < n // 2 else 2 * n - 1 - 2 * k


def ring_links(n):
    right = [(ring_head(n, k), ring_head(n, k + 1)) for k in range(n)]
    return (right, [(b, a) for a, b in right])


def ring_place():
    n = lax.axis_size("head")
    me = lax.axis_index("head")
    odd = me % 2
    return (1 - odd) * (me // 2) + odd * (n - 1 - me // 2)


def head_at(offset):
    n = lax.axis_size("head")
    k = (ring_place() + offset + n) % n
    down = k // (n // 2)
    return (1 - down) * 2 * k + down * (2 * n - 1 - 2 * k)


def gather_ring(block):
    n = lax.axis_size("head")
    right, left = ring_links(n)
    half = n // 2
    rows = block.shape[0] // 2
    out = jnp.zeros((n,) + block.shape, block.dtype)

    def put(out, piece, offset):
        return lax.dynamic_update_slice_in_dim(out, piece[None], head_at(offset), 0)

    out = put(out, block, 0)
    r = l = block
    for step in range(1, half):
        r = lax.ppermute(r, "head", right)
        l = lax.ppermute(l, "head", left)
        out = put(out, r, -step)
        out = put(out, l, step)
    a = lax.ppermute(r[:rows], "head", right)
    b = lax.ppermute(l[rows:], "head", left)
    return put(out, jnp.concatenate([a, b], 0), half)


def scatter_ring(parts):
    n = lax.axis_size("head")
    right, left = ring_links(n)
    half = n // 2
    rows = parts.shape[1] // 2

    def piece(offset):
        return lax.dynamic_index_in_dim(parts, head_at(offset), 0, keepdims=False)

    far = piece(half)
    r = lax.ppermute(far[:rows], "head", right)
    l = lax.ppermute(far[rows:], "head", left)
    for step in range(half - 1, 0, -1):
        br = piece(step).astype(F32)
        bl = piece(-step).astype(F32)
        if step == half - 1:
            br = jnp.concatenate([br[:rows] + r.astype(F32), br[rows:]], 0)
            bl = jnp.concatenate([bl[:rows], bl[rows:] + l.astype(F32)], 0)
        else:
            br = br + r.astype(F32)
            bl = bl + l.astype(F32)
        r = lax.ppermute(br.astype(BF), "head", right)
        l = lax.ppermute(bl.astype(BF), "head", left)
    return piece(0).astype(F32) + r.astype(F32) + l.astype(F32)


def rotate(values, cosine, sine):
    half = HD // 2
    shaped = values.reshape(values.shape[0], -1, HD)
    first = shaped[..., :half]
    second = shaped[..., half:]
    turned = jnp.concatenate(
        [first * cosine - second * sine, second * cosine + first * sine], axis=-1
    )
    return turned.reshape(values.shape)


def dot(a, b, dims=((1,), (0,))):
    return lax.dot_general(a, b, (dims, ((), ())), preferred_element_type=F32)


NT = ((1,), (1,))
TN = ((0,), (0,))


def body(
    hidden,
    w_qkv,
    w_out,
    w_router,
    g_attn,
    g_ffn,
    g_q,
    g_k,
    w_gate,
    w_up,
    w_down,
    lengths,
    routes,
    route_codes,
    cotangent,
):
    n = lax.axis_size("head")
    m = lax.axis_size("fsdp")
    me = lax.axis_index("head")
    rows = hidden.shape[1]
    width = hidden.shape[2]
    seq = rows * n
    lh = HEADS // n
    dh = lh * HD
    experts = EXP_DEV * n
    shard = w_qkv.shape[0]
    scale = 1.0 / math.sqrt(HD)
    both = ("head", "fsdp")
    small = jnp.concatenate(
        [w_router, g_attn[:, None], g_ffn[:, None], g_q[:, None], g_k[:, None]], axis=1
    )
    small = lax.all_gather(small, both, axis=0, tiled=True)
    router = small[:, :experts]
    gain_attn = small[:, experts].astype(F32)
    gain_ffn = small[:, experts + 1].astype(F32)
    gains_q = lax.dynamic_slice_in_dim(small[:, experts + 2], me * dh, dh, 0).astype(F32)
    gains_k = lax.dynamic_slice_in_dim(small[:, experts + 3], me * dh, dh, 0).astype(F32)
    cols = w_qkv.reshape(shard, 3, n, dh).transpose(2, 0, 1, 3).reshape(n, shard, 3 * dh)
    cols = lax.all_to_all(cols, "head", split_axis=0, concat_axis=0, tiled=True)
    qkv = lax.all_gather(cols, "fsdp", axis=1, tiled=True).reshape(width, 3 * dh)
    tokens_all = gather_ring(hidden[0]).reshape(seq, width)
    info = gather_ring(jnp.concatenate([routes[0], route_codes[0]], axis=1)).reshape(seq, 2 * TOP)
    full_out = lax.all_gather(w_out, both, axis=0, tiled=True)
    full_gate = lax.all_gather(w_gate, "fsdp", axis=1, tiled=True)
    full_up = lax.all_gather(w_up, "fsdp", axis=1, tiled=True)
    full_down = lax.all_gather(w_down, "fsdp", axis=1, tiled=True)

    def own(values):
        return lax.dynamic_slice_in_dim(values, me * rows, rows, 0)

    def inverse_rms(values):
        return lax.rsqrt(jnp.mean(values * values, axis=-1, keepdims=True) + EPS)

    wide = tokens_all.astype(F32)
    attn_input = (wide * inverse_rms(wide) * gain_attn).astype(BF)
    projected = dot(attn_input, qkv)
    proj_q = projected[:, :dh]
    proj_k = projected[:, dh : 2 * dh]
    squares = jnp.stack([jnp.sum(proj_q * proj_q, axis=1), jnp.sum(proj_k * proj_k, axis=1)])
    squares = lax.psum(squares, "head") / width
    inv_q = lax.rsqrt(squares[0] + EPS)[:, None]
    inv_k = lax.rsqrt(squares[1] + EPS)[:, None]
    frequency = ROPE_BASE ** (-2.0 * jnp.arange(HD // 2, dtype=F32) / HD)
    angles = jnp.arange(seq, dtype=F32)[:, None] * frequency[None, :]
    cosine = jnp.cos(angles)[:, None, :]
    sine = jnp.sin(angles)[:, None, :]
    queries = rotate(proj_q * inv_q * gains_q, cosine, sine).astype(BF)
    keys = rotate(proj_k * inv_k * gains_k, cosine, sine).astype(BF)
    values = projected[:, 2 * dh :].astype(BF)
    valid = jnp.arange(seq, dtype=jnp.int32) < lengths[0]

    def probs_of(q, k):
        scores = jnp.where(valid[None, :], dot(q, k, NT) * scale, NEGATIVE)
        exponent = jnp.exp(scores - jnp.max(scores, axis=-1, keepdims=True))
        return exponent / jnp.sum(exponent, axis=-1, keepdims=True)

    attended = []
    for head in range(lh):
        part = slice(head * HD, (head + 1) * HD)
        probabilities = probs_of(queries[:, part], keys[:, part]).astype(BF)
        attended.append(dot(probabilities, values[:, part]).astype(BF))
    attended = jnp.concatenate(attended, axis=1)
    attended_all = gather_ring(attended).transpose(1, 0, 2).reshape(seq, width)
    residual = wide + dot(attended_all, full_out)
    inv_ffn = inverse_rms(residual)
    ffn_input = (residual * inv_ffn * gain_ffn).astype(BF)
    logits = dot(ffn_input, router)
    matches = info[:, :TOP, None] == jnp.arange(experts, dtype=jnp.int32)[None, None, :]
    chosen = (
        jnp.sum(jnp.where(matches, logits[:, None, :], 0.0), axis=-1)
        + info[:, TOP:].astype(F32) / 1024.0
    )
    chosen = jnp.exp(chosen - jnp.max(chosen, axis=1, keepdims=True))
    gates = chosen / jnp.sum(chosen, axis=1, keepdims=True)
    spread = jnp.sum(jnp.where(matches, gates[:, :, None], 0.0), axis=1)
    mine = lax.dynamic_slice_in_dim(spread, me * EXP_DEV, EXP_DEV, 1)
    cot_all = gather_ring(cotangent[0]).reshape(seq, width)
    mixed = jnp.zeros((seq, width), F32)
    grad_in = jnp.zeros((seq, width), F32)
    gate_dots, gate_grads, up_grads, down_grads = ([], [], [], [])
    for e in range(EXP_DEV):
        gate = mine[:, e : e + 1]
        gate_pre = dot(ffn_input, full_gate[e])
        up_pre = dot(ffn_input, full_up[e])
        sig = jax.nn.sigmoid(gate_pre)
        silu = gate_pre * sig
        act = (silu * up_pre).astype(BF)
        produced = dot(act, full_down[e]).astype(BF).astype(F32)
        mixed = mixed + gate * produced
        cot_f = cot_all.astype(F32)
        gate_dots.append(jnp.sum(produced * cot_f, axis=1))
        grad_out = (gate * cot_f).astype(BF)
        grad_act = dot(grad_out, full_down[e], NT)
        grad_gate_pre = (grad_act * up_pre * sig * (1.0 + gate_pre * (1.0 - sig))).astype(BF)
        grad_up_pre = (grad_act * silu).astype(BF)
        down_grads.append(dot(act, grad_out, TN).astype(BF))
        gate_grads.append(dot(ffn_input, grad_gate_pre, TN).astype(BF))
        up_grads.append(dot(ffn_input, grad_up_pre, TN).astype(BF))
        grad_in = grad_in + dot(grad_gate_pre, full_gate[e], NT) + dot(grad_up_pre, full_up[e], NT)
    grad_ffn = scatter_ring(grad_in.astype(BF).reshape(n, rows, width))
    summed = scatter_ring(mixed.astype(BF).reshape(n, rows, width))

    def over_fsdp(grads):
        return lax.psum_scatter(jnp.stack(grads), "fsdp", scatter_dimension=1, tiled=True).astype(
            F32
        )

    grad_w_gate = over_fsdp(gate_grads)
    grad_w_up = over_fsdp(up_grads)
    grad_w_down = over_fsdp(down_grads)
    dots = jnp.stack(gate_dots).reshape(EXP_DEV, n, rows).transpose(1, 0, 2)
    dots = lax.all_to_all(dots, "head", split_axis=0, concat_axis=0, tiled=True)
    dots = dots.reshape(experts, rows).T
    own_spread = own(spread)
    own_residual = own(residual)
    out_rows = own_residual + summed
    grad_rows = cotangent[0].astype(F32)
    grad_logits = own_spread * (dots - jnp.sum(own_spread * dots, axis=1, keepdims=True))
    high = lax.Precision.HIGHEST
    grad_ffn = grad_ffn + jnp.dot(grad_logits, router.astype(F32).T, precision=high)
    grad_router = jnp.dot(own(ffn_input).astype(F32).T, grad_logits, precision=high)

    def norm_back(values, gain, grad):
        inv = inverse_rms(values)
        unit = values * inv
        scaled = grad * gain
        back = inv * (scaled - unit * jnp.mean(scaled * unit, axis=-1, keepdims=True))
        return (back, jnp.sum(grad * unit, axis=0))

    back, grad_gain_ffn = norm_back(own_residual, gain_ffn, grad_ffn)
    grad_residual = grad_rows + back
    grad_attn_out = grad_residual.astype(BF)
    grad_attended = dot(grad_attn_out, full_out, NT).astype(BF)
    grad_heads = lax.all_to_all(
        grad_attended.reshape(rows, n, dh), "head", split_axis=1, concat_axis=0, tiled=True
    ).reshape(seq, dh)
    grad_q, grad_k, grad_v = ([], [], [])
    for head in range(lh):
        part = slice(head * HD, (head + 1) * HD)
        probabilities = probs_of(queries[:, part], keys[:, part])
        grad_probs = dot(grad_heads[:, part], values[:, part], NT)
        inner = jnp.sum(probabilities * grad_probs, axis=-1, keepdims=True)
        grad_scores = (probabilities * (grad_probs - inner)).astype(BF)
        grad_q.append((dot(grad_scores, keys[:, part]) * scale).astype(BF))
        grad_k.append((dot(grad_scores, queries[:, part], TN) * scale).astype(BF))
        grad_v.append(dot(probabilities.astype(BF), grad_heads[:, part], TN).astype(BF))
    turned_q = rotate(jnp.concatenate(grad_q, axis=1).astype(F32), cosine, -sine)
    turned_k = rotate(jnp.concatenate(grad_k, axis=1).astype(F32), cosine, -sine)
    unit_q = proj_q * inv_q
    unit_k = proj_k * inv_k
    means = jnp.stack(
        [jnp.sum(turned_q * gains_q * unit_q, axis=1), jnp.sum(turned_k * gains_k * unit_k, axis=1)]
    )
    means = lax.psum(means, "head") / width
    grad_projected = jnp.concatenate(
        [
            (inv_q * (turned_q * gains_q - unit_q * means[0][:, None])).astype(BF),
            (inv_k * (turned_k * gains_k - unit_k * means[1][:, None])).astype(BF),
            jnp.concatenate(grad_v, axis=1),
        ],
        axis=1,
    )
    grad_gain_q = jnp.sum(turned_q * unit_q, axis=0)
    grad_gain_k = jnp.sum(turned_k * unit_k, axis=0)
    grad_attn_in = dot(grad_projected, qkv, NT).astype(BF)
    grad_attn_in = scatter_ring(grad_attn_in.reshape(n, rows, width))
    grad_qkv = dot(attn_input, grad_projected, TN).astype(BF).reshape(n, m * shard, 3 * dh)
    grad_qkv = lax.psum_scatter(grad_qkv, "fsdp", scatter_dimension=1, tiled=True)
    grad_qkv = lax.all_to_all(grad_qkv, "head", split_axis=0, concat_axis=0, tiled=True)
    grad_qkv = grad_qkv.reshape(n, shard, 3, dh).transpose(1, 2, 0, 3).reshape(shard, 3 * width)
    grad_all = gather_ring(grad_attn_out).reshape(seq, width)
    grad_out_w = dot(attended, grad_all, TN)
    grad_out_w = lax.psum_scatter(grad_out_w, "fsdp", scatter_dimension=0, tiled=True)
    back, grad_gain_attn = norm_back(hidden[0].astype(F32), gain_attn, grad_attn_in)
    grad_hidden = grad_residual + back

    def at_mine(piece):
        return lax.dynamic_update_slice_in_dim(jnp.zeros((width,), F32), piece, me * dh, 0)[:, None]

    pack = jnp.concatenate(
        [
            grad_router,
            grad_gain_attn[:, None],
            grad_gain_ffn[:, None],
            at_mine(grad_gain_q),
            at_mine(grad_gain_k),
        ],
        axis=1,
    ).reshape(n * m, shard * (experts + 4))
    pack = lax.all_to_all(pack, both, split_axis=0, concat_axis=0, tiled=True)
    pack = jnp.sum(pack, axis=0).reshape(shard, experts + 4)
    return (
        out_rows.astype(BF)[None],
        grad_hidden[None],
        grad_qkv.astype(F32),
        grad_out_w,
        pack[:, :experts],
        pack[:, experts],
        pack[:, experts + 1],
        pack[:, experts + 2],
        pack[:, experts + 3],
        grad_w_gate,
        grad_w_up,
        grad_w_down,
    )


def solution(mesh):
    both = ("head", "fsdp")
    return jax.shard_map(
        body,
        mesh=mesh,
        in_specs=(
            P("fsdp", "head", None),
            P(both, None),
            P(both, None),
            P(both, None),
            P(both),
            P(both),
            P(both),
            P(both),
            P("head", "fsdp", None),
            P("head", "fsdp", None),
            P("head", "fsdp", None),
            P("fsdp"),
            P("fsdp", "head", None),
            P("fsdp", "head", None),
            P("fsdp", "head", None),
        ),
        out_specs=(
            P("fsdp", "head", None),
            P("fsdp", "head", None),
            P(both, None),
            P(both, None),
            P(both, None),
            P(both),
            P(both),
            P(both),
            P(both),
            P("head", "fsdp", None),
            P("head", "fsdp", None),
            P("head", "fsdp", None),
        ),
        check_vma=False,
    )
```

profile of v0, /device:TPU:0, one launch (start us, length us, event | category | flops | bytes accessed | tf_op | source)
XLA Modules:
  0.0 871.2 jit_solution(12422500406623019625)
XLA Ops:
  10.0 27.5 %all_to_all.40 = bf16[8,64,768]{2,1,0:T(8,128)(2,1)} all-to-all(bf16[8,64,768]{2,1,0:T(8,128)(2,1)S(1)} %reshape.375), channel_id=1, replica_groups=mesh['head'=8,'fsdp'=4] {'head'}, dimensions={0} | all-to-all | bytes 1572864 | tf_op jit(solution)/shard_map/all_to_all | solution.py:149
  45.0 53.5 %all-gather = bf16[32,64,20]{1,2,0:T(8,128)(2,1)S(1)} all-gather(bf16[1,64,20]{1,2,0:T(8,128)(2,1)S(1)} %bitcast.496), channel_id=1, replica_groups=mesh['head'=8,'fsdp'=4] {'head','fsdp'}, dimensions={0}, use_global_device_ids=true | all-gather | bytes 84480 | tf_op jit(solution)/shard_map/all_gather | solution.py:142
  127.1 25.3 %collective-permute-done.33 = bf16[128,2048]{1,0:T(8,128)(2,1)} collective-permute-done((bf16[128,2048]{1,0:T(8,128)(2,1)S(1)}, bf16[128,2048]{1,0:T(8,128)(2,1)}, u32[]{:S(2)}, u32[]{:S(2)}) %collective-permute-start.33) | collective-permute-done | bytes 524320 | tf_op jit(solution)/shard_map/ppermute | solution.py:57
  167.3 8.4 collective-permute-done.35
  179.5 7.4 collective-permute-done.5
  190.6 7.6 collective-permute-done.37
  213.6 7.9 fusion.132
  221.7 20.3 %psum.14 = f32[2,1024]{1,0:T(2,128)} all-reduce(f32[2,1024]{1,0:T(2,128)S(1)} %pad_maximum_fusion.17), channel_id=1, replica_groups=mesh['head'=8,'fsdp'=4] {'head'}, use_global_device_ids=true, to_apply=%region_3.4 | all-reduce | flops 2048 | bytes 16384 | tf_op jit(solution)/shard_map/psum | solution.py:170
  258.6 10.1 %collective-permute-done.8 = bf16[1024,256]{0,1:T(8,128)(2,1)S(1)} collective-permute-done((bf16[1024,256]{0,1:T(8,128)(2,1)S(1)}, bf16[1024,256]{0,1:T(8,128)(2,1)S(1)}, u32[]{:S(2)}, u32[]{:S(2)}) %collective-permute-start.8) | collective-permute-done | bytes 524320 | tf_op jit(solution)/shard_map/ppermute | solution.py:56
  302.5 14.3 %multiply_reduce_fusion = (f32[1024]{0:T(1024)S(1)}, f32[1024,2048]{1,0:T(8,128)S(1)}) fusion(bf16[1024,2048]{0,1:T(8,128)(2,1)} %bitcast.38, bf16[2048,2048]{1,0:T(8,128)(2,1)} %all-gather.9.cloned.1.call-done, bf16[8,128,2048]{2,1,0:T(8,128)(2,1)} %fusion.75), kind=kOutput, calls=%fused_computation.30 | convolution fusion | flops 8598322176 | bytes 25169920 | tf_op jit(solution)/shard_map/dot_general | solution.py:103
  329.3 10.0 %fusion.18 = f32[1024,1024]{1,0:T(8,128)} fusion(bf16[1024,2048]{1,0:T(8,128)(2,1)} %copy-done.6, bf16[2,2048,1024]{2,1,0:T(8,128)(2,1)} %all-gather.11.cloned.1.call-done), kind=kOutput, calls=%fused_computation.67 | convolution fusion | flops 4294967296 | bytes 12582912 | tf_op jit(solution)/shard_map/dot_general | solution.py:103
  345.8 10.0 %fusion.20 = f32[1024,1024]{1,0:T(8,128)} fusion(bf16[1024,2048]{1,0:T(8,128)(2,1)} %copy-done.6, bf16[2,2048,1024]{2,1,0:T(8,128)(2,1)} %all-gather.13.cloned.1.call-done), kind=kOutput, calls=%fused_computation.69 | convolution fusion | flops 4294967296 | bytes 12582912 | tf_op jit(solution)/shard_map/dot_general | solution.py:103
  362.0 12.2 %multiply_convert_fusion.5 = (bf16[1024,1024]{1,0:T(8,128)(2,1)S(1)}, bf16[1024,1024]{1,0:T(8,128)(2,1)S(1)}, bf16[1024,1024]{1,0:T(8,128)(2,1)}) fusion(f32[1024,1024]{1,0:T(8,128)} %fusion.18, f32[1024,1024]{1,0:T(8,128)} %fusion.20, bf16[1024,2048]{1,0:T(8,128)(2,1)} %bitcast.454, bf16[2,1024,2048]{2,1,0:T(8,128)(2,1)} %all-gather.15.cloned.1.call-done), kind=kOutput, calls=%fused_computation.49 | convolution fusion | flops 4310695936 | bytes 23068672 | tf_op jit(solution)/shard_map/dot_general | solution.py:103
  374.2 10.4 %fusion.17 = f32[1024,2048]{1,0:T(8,128)} fusion(bf16[1024,1024]{1,0:T(8,128)(2,1)S(1)} %get-tuple-element.89, bf16[2,2048,1024]{2,1,0:T(8,128)(2,1)} %all-gather.11.cloned.1.call-done), kind=kOutput, calls=%fused_computation.66 | convolution fusion | flops 4294967296 | bytes 14680064 | tf_op jit(solution)/shard_map/dot_general | solution.py:103
  384.7 9.1 %fusion.19 = f32[1024,2048]{1,0:T(8,128)} fusion(bf16[1024,1024]{1,0:T(8,128)(2,1)S(1)} %get-tuple-element.88, bf16[2,2048,1024]{2,1,0:T(8,128)(2,1)} %all-gather.13.cloned.1.call-done), kind=kOutput, calls=%fused_computation.68 | convolution fusion | flops 4294967296 | bytes 14680064 | tf_op jit(solution)/shard_map/dot_general | solution.py:103
  393.8 10.4 %multiply_convert_fusion.3 = (bf16[1024,1024]{1,0:T(8,128)(2,1)S(1)}, bf16[1024,1024]{1,0:T(8,128)(2,1)}, bf16[1024,1024]{1,0:T(8,128)(2,1)}) fusion(f32[1024,1024]{1,0:T(8,128)} %fusion.23, f32[1024,1024]{1,0:T(8,128)} %fusion.24, bf16[1024,2048]{1,0:T(8,128)(2,1)S(1)} %bitcast.453, bf16[2,1024,2048]{2,1,0:T(8,128)(2,1)S(1)} %bitcast.530), kind=kOutput, calls=%fused_computation.47 | convolution fusion | flops 4310695936 | bytes 23068672 | tf_op jit(solution)/shard_map/dot_general | solution.py:103
  404.2 9.1 %fusion.22 = f32[1024,2048]{1,0:T(8,128)} fusion(bf16[1024,1024]{1,0:T(8,128)(2,1)} %get-tuple-element.86, bf16[2,2048,1024]{2,1,0:T(8,128)(2,1)S(1)} %bitcast.532), kind=kOutput, calls=%fused_computation.71 | convolution fusion | flops 4294967296 | bytes 14680064 | tf_op jit(solution)/shard_map/dot_general | solution.py:103
  413.4 13.3 %add_convert_fusion = bf16[1024,2048]{1,0:T(8,128)(2,1)} fusion(f32[1024,2048]{1,0:T(8,128)} %fusion.22, f32[1024,2048]{1,0:T(8,128)} %fusion.17, f32[1024,2048]{1,0:T(8,128)} %fusion.19, bf16[1024,1024]{1,0:T(8,128)(2,1)S(1)} %get-tuple-element.85, bf16[2,2048,1024]{2,1,0:T(8,128)(2,1)} %all-gather.13.cloned.1.call-done), kind=kOutput, calls=%fused_computation.28 | convolution fusion | flops 4303355904 | bytes 35651584 | tf_op jit(solution)/shard_map/dot_general | solution.py:103
  440.5 11.3 %collective-permute-done.41 = bf16[128,2048]{1,0:T(8,128)(2,1)S(1)} collective-permute-done((bf16[128,2048]{1,0:T(8,128)(2,1)S(1)}, bf16[128,2048]{1,0:T(8,128)(2,1)S(1)}, u32[]{:S(2)}, u32[]{:S(2)}) %collective-permute-start.41) | collective-permute-done | bytes 524320 | tf_op jit(solution)/shard_map/ppermute | solution.py:86
  453.3 7.5 convolution_convert_fusion.1
  465.8 12.6 %fusion.2 = (f32[1024]{0:T(1024)S(1)}, f32[1024]{0:T(1024)S(1)}, bf16[1024,2048]{1,0:T(8,128)(2,1)}, bf16[1024,2048]{1,0:T(8,128)(2,1)}, bf16[1024,2048]{1,0:T(8,128)(2,1)}) fusion(bf16[8,128,2048]{2,1,0:T(8,128)(2,1)} %fusion.77, bf16[1024,2048]{1,0:T(8,128)(2,1)S(1)} %convolution_convert_fusion.1, f32[1024]{0:T(1024)S(1)} %bitcast.500, ...), kind=kOutput, calls=%fused_computation.6 | convolution fusion | flops 4328519680 | bytes 27279360 | tf_op jit(solution)/shard_map/dot_general | solution.py:103
  542.8 19.8 %psum.15 = f32[2,1024]{1,0:T(2,128)S(1)} all-reduce(f32[2,1024]{1,0:T(2,128)S(1)} %pad_maximum_fusion.18), channel_id=1, replica_groups=mesh['head'=8,'fsdp'=4] {'head'}, use_global_device_ids=true, to_apply=%region_23.24 | all-reduce | flops 2048 | bytes 16384 | tf_op jit(solution)/shard_map/psum | solution.py:284
  570.6 7.6 convert_bitcast_fusion.1
  590.9 7.6 convert_bitcast_fusion.3
  613.1 7.7 convert_bitcast_fusion.5
  647.4 7.6 collective-permute-done.56
  663.5 11.3 %collective-permute-done.58 = bf16[128,2048]{1,0:T(8,128)(2,1)S(1)} collective-permute-done((bf16[128,2048]{1,0:T(8,128)(2,1)S(1)}, bf16[128,2048]{1,0:T(8,128)(2,1)S(1)}, u32[]{:S(2)}, u32[]{:S(2)}) %collective-permute-start.58) | collective-permute-done | bytes 524320 | tf_op jit(solution)/shard_map/ppermute | solution.py:56
  681.4 7.4 collective-permute-done.60
  691.8 8.3 collective-permute-done.49
  762.2 23.2 %collective-permute-done.31 = bf16[128,2048]{1,0:T(8,128)(2,1)S(1)} collective-permute-done((bf16[128,2048]{1,0:T(8,128)(2,1)S(1)}, bf16[128,2048]{1,0:T(8,128)(2,1)S(1)}, u32[]{:S(2)}, u32[]{:S(2)}) %collective-permute-start.31) | collective-permute-done | bytes 524320 | tf_op jit(solution)/shard_map/ppermute | solution.py:87
  802.9 26.6 %reduce-scatter.10.cloned.1.call-done = bf16[2,512,1024]{2,1,0:T(8,128)(2,1)} async-done(((bf16[2,2048,1024]{2,1,0:T(8,128)(2,1)}), bf16[2,512,1024]{2,1,0:T(8,128)(2,1)}) %reduce-scatter.10.cloned.1.call-update) | async-done | bytes 2097168 | tf_op jit(solution)/shard_map/reduce_scatter | solution.py:234
  833.5 30.4 %reduce-scatter.8.cloned.1.call-done = f32[64,2048]{1,0:T(8,128)} async-done(((f32[256,2048]{1,0:T(8,128)}), f32[64,2048]{1,0:T(8,128)}) %reduce-scatter.8.cloned.1.call-update) | async-done | bytes 524304 | tf_op jit(solution)/shard_map/reduce_scatter | solution.py:303
  (527 shorter events, 398.2 us)
Async XLA Ops:
  7.2 206.4 %all-gather.7.cloned.1.call-start = ((), (), s32[]{:S(2)}) async-start(), calls=%async_computation.10 | async-start | bytes 3932160 | tf_op jit(solution)/shard_map/all_gather | solution.py:150
  37.5 265.0 %all-gather.9.cloned.1.call-start = ((), (), s32[]{:S(2)}) async-start(), calls=%async_computation.11 | async-start | bytes 8650752 | tf_op jit(solution)/shard_map/all_gather | solution.py:153
  38.2 291.1 %all-gather.11.cloned.1.call-start = ((), (), s32[]{:S(2)}) async-start(), calls=%async_computation.12 | async-start | bytes 10485760 | tf_op jit(solution)/shard_map/all_gather | solution.py:154
  39.0 306.8 %all-gather.13.cloned.1.call-start = ((), (), s32[]{:S(2)}) async-start(), calls=%async_computation.13 | async-start | bytes 10485760 | tf_op jit(solution)/shard_map/all_gather | solution.py:155
  39.5 322.5 %all-gather.15.cloned.1.call-start = ((), (), s32[]{:S(2)}) async-start(), calls=%async_computation.14 | async-start | bytes 10485760 | tf_op jit(solution)/shard_map/all_gather | solution.py:156
  39.6 69.0 %collective-permute-start.16 = (s32[128,16]{0,1:T(8,128)S(1)}, s32[128,16]{0,1:T(8,128)S(1)}, u32[]{:S(2)}, u32[]{:S(2)}) collective-permute-start(s32[128,16]{0,1:T(8,128)S(1)} %pad_add_fusion), channel_id=1, source_target_pairs={{0,8},{8,16},{16,24},{24,28},{28,20},{20,12},{12,4},{4,0},{1,9},{9... | collective-permute-start | bytes 24584 | tf_op jit(solution)/shard_map/ppermute | solution.py:56
  40.8 67.9 %collective-permute-start.17 = (s32[128,16]{0,1:T(8,128)S(1)}, s32[128,16]{0,1:T(8,128)S(1)}, u32[]{:S(2)}, u32[]{:S(2)}) collective-permute-start(s32[128,16]{0,1:T(8,128)S(1)} %pad_add_fusion), channel_id=1, source_target_pairs={{8,0},{16,8},{24,16},{28,24},{20,28},{12,20},{4,12},{0,4},{9,1},{1... | collective-permute-start | bytes 24584 | tf_op jit(solution)/shard_map/ppermute | solution.py:57
  41.7 80.4 %collective-permute-start = (bf16[128,2048]{1,0:T(8,128)(2,1)S(1)}, bf16[128,2048]{1,0:T(8,128)(2,1)S(1)}, u32[]{:S(2)}, u32[]{:S(2)}) collective-permute-start(bf16[128,2048]{1,0:T(8,128)(2,1)S(1)} %bitcast.420), channel_id=1, source_target_pairs={{0,8},{8,16},{16,24},{24,28},{28,20},{20,12},{12,4},{4,0},{1,9},{9... | collective-permute-start | bytes 1572872 | tf_op jit(solution)/shard_map/ppermute | solution.py:56
  42.8 80.6 %collective-permute-start.1 = (bf16[128,2048]{1,0:T(8,128)(2,1)S(1)}, bf16[128,2048]{1,0:T(8,128)(2,1)S(1)}, u32[]{:S(2)}, u32[]{:S(2)}) collective-permute-start(bf16[128,2048]{1,0:T(8,128)(2,1)S(1)} %bitcast.421), channel_id=1, source_target_pairs={{8,0},{16,8},{24,16},{28,24},{20,28},{12,20},{4,12},{0,4},{9,1},{1... | collective-permute-start | bytes 1572872 | tf_op jit(solution)/shard_map/ppermute | solution.py:57
  43.7 82.2 %collective-permute-start.32 = (bf16[128,2048]{1,0:T(8,128)(2,1)S(1)}, bf16[128,2048]{1,0:T(8,128)(2,1)S(1)}, u32[]{:S(2)}, u32[]{:S(2)}) collective-permute-start(bf16[128,2048]{1,0:T(8,128)(2,1)S(1)} %bitcast.434), channel_id=1, source_target_pairs={{0,8},{8,16},{16,24},{24,28},{28,20},{20,12},{12,4},{4,0},{1,9},{9... | collective-permute-start | bytes 1572872 | tf_op jit(solution)/shard_map/ppermute | solution.py:56
  120.3 32.1 %collective-permute-start.33 = (bf16[128,2048]{1,0:T(8,128)(2,1)S(1)}, bf16[128,2048]{1,0:T(8,128)(2,1)}, u32[]{:S(2)}, u32[]{:S(2)}) collective-permute-start(bf16[128,2048]{1,0:T(8,128)(2,1)S(1)} %bitcast.435), channel_id=1, source_target_pairs={{8,0},{16,8},{24,16},{28,24},{20,28},{12,20},{4,12},{0,4},{9,1},{1... | collective-permute-start | bytes 1572872 | tf_op jit(solution)/shard_map/ppermute | solution.py:57
  122.2 32.2 %collective-permute-start.2 = (bf16[128,2048]{1,0:T(8,128)(2,1)S(1)}, bf16[128,2048]{1,0:T(8,128)(2,1)S(1)}, u32[]{:S(2)}, u32[]{:S(2)}) collective-permute-start(bf16[128,2048]{1,0:T(8,128)(2,1)S(1)} %collective-permute-done), channel_id=1, source_target_pairs={{0,8},{8,16},{16,24},{24,28},{28,20},{20,12},{12,4},{4,0},{1,9},{9... | collective-permute-start | bytes 1572872 | tf_op jit(solution)/shard_map/ppermute | solution.py:56
  123.4 41.0 %collective-permute-start.3 = (bf16[128,2048]{1,0:T(8,128)(2,1)S(1)}, bf16[128,2048]{1,0:T(8,128)(2,1)S(1)}, u32[]{:S(2)}, u32[]{:S(2)}) collective-permute-start(bf16[128,2048]{1,0:T(8,128)(2,1)S(1)} %collective-permute-done.1), channel_id=1, source_target_pairs={{8,0},{16,8},{24,16},{28,24},{20,28},{12,20},{4,12},{0,4},{9,1},{1... | collective-permute-start | bytes 1572872 | tf_op jit(solution)/shard_map/ppermute | solution.py:57
  125.9 38.7 %collective-permute-start.34 = (bf16[128,2048]{1,0:T(8,128)(2,1)S(1)}, bf16[128,2048]{1,0:T(8,128)(2,1)S(1)}, u32[]{:S(2)}, u32[]{:S(2)}) collective-permute-start(bf16[128,2048]{1,0:T(8,128)(2,1)S(1)} %collective-permute-done.32), channel_id=1, source_target_pairs={{0,8},{8,16},{16,24},{24,28},{28,20},{20,12},{12,4},{4,0},{1,9},{9... | collective-permute-start | bytes 1572872 | tf_op jit(solution)/shard_map/ppermute | solution.py:56
  152.4 23.3 %collective-permute-start.35 = (bf16[128,2048]{1,0:T(8,128)(2,1)}, bf16[128,2048]{1,0:T(8,128)(2,1)S(1)}, u32[]{:S(2)}, u32[]{:S(2)}) collective-permute-start(bf16[128,2048]{1,0:T(8,128)(2,1)} %collective-permute-done.33), channel_id=1, source_target_pairs={{8,0},{16,8},{24,16},{28,24},{20,28},{12,20},{4,12},{0,4},{9,1},{1... | collective-permute-start | bytes 1572872 | tf_op jit(solution)/shard_map/ppermute | solution.py:57
  154.3 23.2 %collective-permute-start.4 = (bf16[128,2048]{1,0:T(8,128)(2,1)S(1)}, bf16[128,2048]{1,0:T(8,128)(2,1)S(1)}, u32[]{:S(2)}, u32[]{:S(2)}) collective-permute-start(bf16[128,2048]{1,0:T(8,128)(2,1)S(1)} %collective-permute-done.2), channel_id=1, source_target_pairs={{0,8},{8,16},{16,24},{24,28},{28,20},{20,12},{12,4},{4,0},{1,9},{9... | collective-permute-start | bytes 1572872 | tf_op jit(solution)/shard_map/ppermute | solution.py:56
  164.5 22.5 %collective-permute-start.5 = (bf16[128,2048]{1,0:T(8,128)(2,1)S(1)}, bf16[128,2048]{1,0:T(8,128)(2,1)S(1)}, u32[]{:S(2)}, u32[]{:S(2)}) collective-permute-start(bf16[128,2048]{1,0:T(8,128)(2,1)S(1)} %collective-permute-done.3), channel_id=1, source_target_pairs={{8,0},{16,8},{24,16},{28,24},{20,28},{12,20},{4,12},{0,4},{9,1},{1... | collective-permute-start | bytes 1572872 | tf_op jit(solution)/shard_map/ppermute | solution.py:57
  164.6 22.5 %collective-permute-start.36 = (bf16[128,2048]{1,0:T(8,128)(2,1)S(1)}, bf16[128,2048]{1,0:T(8,128)(2,1)S(1)}, u32[]{:S(2)}, u32[]{:S(2)}) collective-permute-start(bf16[128,2048]{1,0:T(8,128)(2,1)S(1)} %collective-permute-done.34), channel_id=1, source_target_pairs={{0,8},{8,16},{16,24},{24,28},{28,20},{20,12},{12,4},{4,0},{1,9},{9... | collective-permute-start | bytes 1572872 | tf_op jit(solution)/shard_map/ppermute | solution.py:56
  177.6 24.3 %collective-permute-start.6 = (bf16[64,2048]{1,0:T(8,128)(2,1)S(1)}, bf16[64,2048]{1,0:T(8,128)(2,1)S(1)}, u32[]{:S(2)}, u32[]{:S(2)}) collective-permute-start(bf16[64,2048]{1,0:T(8,128)(2,1)S(1)} %slice.410), channel_id=1, source_target_pairs={{0,8},{8,16},{16,24},{24,28},{28,20},{20,12},{12,4},{4,0},{1,9},{9... | collective-permute-start | bytes 786440 | tf_op jit(solution)/shard_map/ppermute | solution.py:60
  188.6 82.4 %collective-permute-start.38 = (bf16[64,2048]{1,0:T(8,128)(2,1)}, bf16[64,2048]{1,0:T(8,128)(2,1)}, u32[]{:S(2)}, u32[]{:S(2)}) collective-permute-start(bf16[64,2048]{1,0:T(8,128)(2,1)} %slice.443), channel_id=1, source_target_pairs={{0,8},{8,16},{16,24},{24,28},{28,20},{20,12},{12,4},{4,0},{1,9},{9... | collective-permute-start | bytes 786440 | tf_op jit(solution)/shard_map/ppermute | solution.py:60
  199.7 71.3 %collective-permute-start.39 = (bf16[64,2048]{1,0:T(8,128)(2,1)}, bf16[64,2048]{1,0:T(8,128)(2,1)}, u32[]{:S(2)}, u32[]{:S(2)}) collective-permute-start(bf16[64,2048]{1,0:T(8,128)(2,1)} %slice.444), channel_id=1, source_target_pairs={{8,0},{16,8},{24,16},{28,24},{20,28},{12,20},{4,12},{0,4},{9,1},{1... | collective-permute-start | bytes 786440 | tf_op jit(solution)/shard_map/ppermute | solution.py:61
  514.4 240.0 %reduce-scatter.6.cloned.1.call-start = ((), (), s32[]{:S(2)}) async-start(), calls=%async_computation.15 | async-start | bytes 3932160 | tf_op jit(solution)/shard_map/reduce_scatter | solution.py:298
  570.4 224.3 %reduce-scatter.14.cloned.1.call-start = ((), (), s32[]{:S(2)}) async-start(), calls=%async_computation.19 | async-start | bytes 10485760 | tf_op jit(solution)/shard_map/reduce_scatter | solution.py:234
  590.8 208.0 %reduce-scatter.12.cloned.1.call-start = ((), (), s32[]{:S(2)}) async-start(), calls=%async_computation.18 | async-start | bytes 10485760 | tf_op jit(solution)/shard_map/reduce_scatter | solution.py:234
  611.2 218.3 %reduce-scatter.10.cloned.1.call-start = ((), (), s32[]{:S(2)}) async-start(), calls=%async_computation.17 | async-start | bytes 10485760 | tf_op jit(solution)/shard_map/reduce_scatter | solution.py:234
  633.2 230.7 %reduce-scatter.8.cloned.1.call-start = ((), (), s32[]{:S(2)}) async-start(), calls=%async_computation.16 | async-start | bytes 2621440 | tf_op jit(solution)/shard_map/reduce_scatter | solution.py:303
  645.2 85.1 %collective-permute-start.29 = (bf16[128,2048]{1,0:T(8,128)(2,1)S(1)}, bf16[128,2048]{1,0:T(8,128)(2,1)}, u32[]{:S(2)}, u32[]{:S(2)}) collective-permute-start(bf16[128,2048]{1,0:T(8,128)(2,1)S(1)} %pad_maximum_fusion.10), channel_id=1, source_target_pairs={{8,0},{16,8},{24,16},{28,24},{20,28},{12,20},{4,12},{0,4},{9,1},{1... | collective-permute-start | bytes 1572872 | tf_op jit(solution)/shard_map/ppermute | solution.py:87
  645.4 74.5 %collective-permute-start.25 = (bf16[128,2048]{1,0:T(8,128)(2,1)S(1)}, bf16[128,2048]{1,0:T(8,128)(2,1)S(1)}, u32[]{:S(2)}, u32[]{:S(2)}) collective-permute-start(bf16[128,2048]{1,0:T(8,128)(2,1)S(1)} %pad_maximum_fusion.9), channel_id=1, source_target_pairs={{0,8},{8,16},{16,24},{24,28},{28,20},{20,12},{12,4},{4,0},{1,9},{9... | collective-permute-start | bytes 1572872 | tf_op jit(solution)/shard_map/ppermute | solution.py:86
  681.3 30.7 %collective-permute-start.53 = (bf16[128,2048]{1,0:T(8,128)(2,1)S(1)}, bf16[128,2048]{1,0:T(8,128)(2,1)}, u32[]{:S(2)}, u32[]{:S(2)}) collective-permute-start(bf16[128,2048]{1,0:T(8,128)(2,1)S(1)} %pad_maximum_fusion.14), channel_id=1, source_target_pairs={{8,0},{16,8},{24,16},{28,24},{20,28},{12,20},{4,12},{0,4},{9,1},{1... | collective-permute-start | bytes 1572872 | tf_op jit(solution)/shard_map/ppermute | solution.py:87
  733.4 24.5 %collective-permute-start.30 = (bf16[128,2048]{1,0:T(8,128)(2,1)}, bf16[128,2048]{1,0:T(8,128)(2,1)}, u32[]{:S(2)}, u32[]{:S(2)}) collective-permute-start(bf16[128,2048]{1,0:T(8,128)(2,1)} %get-tuple-element.113), channel_id=1, source_target_pairs={{8,0},{16,8},{24,16},{28,24},{20,28},{12,20},{4,12},{0,4},{9,1},{1... | collective-permute-start | bytes 1572872 | tf_op jit(solution)/shard_map/ppermute | solution.py:87
  754.4 36.8 %all-to-all-start.3 = ((bf16[8,64,768]{2,1,0:T(8,128)(2,1)}), bf16[8,64,768]{2,1,0:T(8,128)(2,1)S(1)}, u32[]{:S(2)}, u32[]{:S(2)}) async-start(bf16[8,64,768]{2,1,0:T(8,128)(2,1)} %reduce-scatter.6.cloned.1.call-done), calls=%async_computation.4 | async-start | bytes 1572864 | tf_op jit(solution)/shard_map/all_to_all | solution.py:299
  759.3 26.1 %collective-permute-start.31 = (bf16[128,2048]{1,0:T(8,128)(2,1)S(1)}, bf16[128,2048]{1,0:T(8,128)(2,1)S(1)}, u32[]{:S(2)}, u32[]{:S(2)}) collective-permute-start(bf16[128,2048]{1,0:T(8,128)(2,1)S(1)} %fusion.60), channel_id=1, source_target_pairs={{8,0},{16,8},{24,16},{28,24},{20,28},{12,20},{4,12},{0,4},{9,1},{1... | collective-permute-start | bytes 1572872 | tf_op jit(solution)/shard_map/ppermute | solution.py:87
  (141 other events, 2030.4 us)
Sparse Core Ops, SparseCore 0:
  37.6 28.0 all-gather.6
  68.6 92.0 all-gather.8
  162.2 65.0 all-gather.10
  228.8 58.2 all-gather.12
  288.5 58.2 all-gather.14
  570.5 33.8 reduce-scatter.5
  607.1 71.6 reduce-scatter.13
  681.4 73.4 reduce-scatter.11
  757.6 71.7 reduce-scatter.9
  832.4 31.4 reduce-scatter.7
where the time goes:
time: 878 us; the launch traced here: 871 us
  waiting for transfers between devices  278 us (32%)
  matrix products  220 us (25%)
  blocking collectives  121 us (14%)
  other arithmetic  99 us (11%)
  starting transfers between devices  79 us (9%)
  local copies, waits for them, and re-layouts  56.9 us (6%)
  between operations  17.3 us (2%)
    dot_general x37, matrix products, dot(): return lax.dot_general(a, b, (dims, ((), ())), preferred_element_type=F32)  218 us
    ppermute x15, waiting for transfers between devices, gather_ring(): l = lax.ppermute(l, 'head', left)  58.9 us
    all_gather x1, blocking collectives, body(): small = lax.all_gather(small, both, axis=0, tiled=True)  53.5 us
    ppermute x15, waiting for transfers between devices, gather_ring(): r = lax.ppermute(r, 'head', right)  49.1 us
    ppermute x9, waiting for transfers between devices, scatter_ring(): r = lax.ppermute(br.astype(BF), 'head', right)  34.1 us
    ppermute x9, waiting for transfers between devices, scatter_ring(): l = lax.ppermute(bl.astype(BF), 'head', left)  32.8 us
    reduce_scatter x1, waiting for transfers between devices, body(): lax.psum_scatter(grad_out_w, 'fsdp', scatter_dimension=0, tiled=True)  30.4 us
    all_to_all x1, blocking collectives, body(): cols = lax.all_to_all(cols, 'head', split_axis=0, concat_axis=0, tiled=True)  27.5 us
  transfers between devices with their start and end apart: 78, of which 43 were waited for; matrix products, arithmetic and copies ran while one was open for 29% of the time, Pallas kernels for 0%

commit v1 on v0

--- a/solution.py
+++ b/solution.py
@@ -167,7 +167,7 @@
     proj_q = projected[:, :dh]
     proj_k = projected[:, dh : 2 * dh]
     squares = jnp.stack([jnp.sum(proj_q * proj_q, axis=1), jnp.sum(proj_k * proj_k, axis=1)])
-    squares = lax.psum(squares, "head") / width
+    squares = jnp.sum(lax.all_gather(squares, "head"), axis=0) / width
     inv_q = lax.rsqrt(squares[0] + EPS)[:, None]
     inv_k = lax.rsqrt(squares[1] + EPS)[:, None]
     frequency = ROPE_BASE ** (-2.0 * jnp.arange(HD // 2, dtype=F32) / HD)

time: 878 us -> 887 us (1.010)
  blocking collectives: 121 us -> 134 us
    all_gather x0 -> x1, blocking collectives: none -> 33 us  [body(): squares = jnp.sum(lax.all_gather(squares, 'head'), axis=0) / width]
    psum x1 -> x0, blocking collectives: 20.3 us -> none  [body(): squares = lax.psum(squares, 'head') / width]
  transfers between devices with their start and end apart: 78 -> 78, of which waited for: 43 -> 44; matrix products, arithmetic and copies ran while one was open for 29% -> 29% of each run, Pallas kernels for 0% -> 0%
where the time goes in v1:
time: 887 us; the launch traced here: 880 us
  waiting for transfers between devices  279 us (31%)
  matrix products  220 us (25%)
  blocking collectives  134 us (15%)
  other arithmetic  99 us (11%)
  starting transfers between devices  74.9 us (8%)
  local copies, waits for them, and re-layouts  56.9 us (6%)
  between operations  17.1 us (2%)
    dot_general x37, matrix products, dot(): return lax.dot_general(a, b, (dims, ((), ())), preferred_element_type=F32)  218 us
    ppermute x15, waiting for transfers between devices, gather_ring(): l = lax.ppermute(l, 'head', left)  62 us
    all_gather x1, blocking collectives, body(): small = lax.all_gather(small, both, axis=0, tiled=True)  53.5 us
    ppermute x15, waiting for transfers between devices, gather_ring(): r = lax.ppermute(r, 'head', right)  45.6 us
    ppermute x9, waiting for transfers between devices, scatter_ring(): l = lax.ppermute(bl.astype(BF), 'head', left)  34.3 us
    all_gather x1, blocking collectives, body(): squares = jnp.sum(lax.all_gather(squares, 'head'), axis=0) / width  33 us
    ppermute x9, waiting for transfers between devices, scatter_ring(): r = lax.ppermute(br.astype(BF), 'head', right)  31.9 us
    reduce_scatter x1, waiting for transfers between devices, body(): lax.psum_scatter(grad_out_w, 'fsdp', scatter_dimension=0, tiled=True)  30.4 us
  transfers between devices with their start and end apart: 78, of which 44 were waited for; matrix products, arithmetic and copies ran while one was open for 29% of the time, Pallas kernels for 0%

profile of v1, /device:TPU:0, one launch (start us, length us, event | category | flops | bytes accessed | tf_op | source)
XLA Modules:
  0.0 880.3 jit_solution(11524296791437319261)
XLA Ops:
  10.0 27.5 %all_to_all.40 = bf16[8,64,768]{2,1,0:T(8,128)(2,1)} all-to-all(bf16[8,64,768]{2,1,0:T(8,128)(2,1)S(1)} %reshape.375), channel_id=1, replica_groups=mesh['head'=8,'fsdp'=4] {'head'}, dimensions={0} | all-to-all | bytes 1572864 | tf_op jit(solution)/shard_map/all_to_all | solution.py:149
  45.0 53.5 %all-gather.1 = bf16[32,64,20]{1,2,0:T(8,128)(2,1)S(1)} all-gather(bf16[1,64,20]{1,2,0:T(8,128)(2,1)S(1)} %bitcast.498), channel_id=1, replica_groups=mesh['head'=8,'fsdp'=4] {'head','fsdp'}, dimensions={0}, use_global_device_ids=true | all-gather | bytes 84480 | tf_op jit(solution)/shard_map/all_gather | solution.py:142
  127.1 25.3 %collective-permute-done.33 = bf16[128,2048]{1,0:T(8,128)(2,1)} collective-permute-done((bf16[128,2048]{1,0:T(8,128)(2,1)S(1)}, bf16[128,2048]{1,0:T(8,128)(2,1)}, u32[]{:S(2)}, u32[]{:S(2)}) %collective-permute-start.33) | collective-permute-done | bytes 524320 | tf_op jit(solution)/shard_map/ppermute | solution.py:57
  157.2 7.3 collective-permute-done.3
  167.3 8.4 collective-permute-done.35
  179.5 7.4 collective-permute-done.5
  190.6 7.6 collective-permute-done.37
  213.6 7.9 fusion.132
  221.7 33.0 %all-gather.2 = f32[8,2,1024]{2,1,0:T(2,128)} all-gather(f32[1,2,1024]{2,1,0:T(2,128)S(1)} %maximum_bitcast_fusion.4), channel_id=2, replica_groups=mesh['head'=8,'fsdp'=4] {'head'}, dimensions={0}, use_global_device_ids=true | all-gather | bytes 73728 | tf_op jit(solution)/shard_map/all_gather | solution.py:170
  271.3 11.0 %collective-permute-done.8 = bf16[1024,256]{0,1:T(8,128)(2,1)S(1)} collective-permute-done((bf16[1024,256]{0,1:T(8,128)(2,1)S(1)}, bf16[1024,256]{0,1:T(8,128)(2,1)S(1)}, u32[]{:S(2)}, u32[]{:S(2)}) %collective-permute-start.8) | collective-permute-done | bytes 524320 | tf_op jit(solution)/shard_map/ppermute | solution.py:56
  314.9 14.4 %multiply_reduce_fusion = (f32[1024]{0:T(1024)S(1)}, f32[1024,2048]{1,0:T(8,128)S(1)}) fusion(bf16[1024,2048]{0,1:T(8,128)(2,1)} %bitcast.39, bf16[2048,2048]{1,0:T(8,128)(2,1)} %all-gather.11.cloned.1.call-done, bf16[8,128,2048]{2,1,0:T(8,128)(2,1)} %fusion.75), kind=kOutput, calls=%fused_computation.30 | convolution fusion | flops 8598322176 | bytes 25169920 | tf_op jit(solution)/shard_map/dot_general | solution.py:103
  341.8 10.0 %fusion.18 = f32[1024,1024]{1,0:T(8,128)} fusion(bf16[1024,2048]{1,0:T(8,128)(2,1)} %copy-done.6, bf16[2,2048,1024]{2,1,0:T(8,128)(2,1)} %all-gather.13.cloned.1.call-done), kind=kOutput, calls=%fused_computation.67 | convolution fusion | flops 4294967296 | bytes 12582912 | tf_op jit(solution)/shard_map/dot_general | solution.py:103
  358.1 10.0 %fusion.20 = f32[1024,1024]{1,0:T(8,128)} fusion(bf16[1024,2048]{1,0:T(8,128)(2,1)} %copy-done.6, bf16[2,2048,1024]{2,1,0:T(8,128)(2,1)} %all-gather.15.cloned.1.call-done), kind=kOutput, calls=%fused_computation.69 | convolution fusion | flops 4294967296 | bytes 12582912 | tf_op jit(solution)/shard_map/dot_general | solution.py:103
  374.3 12.2 %multiply_convert_fusion.5 = (bf16[1024,1024]{1,0:T(8,128)(2,1)S(1)}, bf16[1024,1024]{1,0:T(8,128)(2,1)S(1)}, bf16[1024,1024]{1,0:T(8,128)(2,1)}) fusion(f32[1024,1024]{1,0:T(8,128)} %fusion.18, f32[1024,1024]{1,0:T(8,128)} %fusion.20, bf16[1024,2048]{1,0:T(8,128)(2,1)} %bitcast.456, bf16[2,1024,2048]{2,1,0:T(8,128)(2,1)} %all-gather.17.cloned.1.call-done), kind=kOutput, calls=%fused_computation.49 | convolution fusion | flops 4310695936 | bytes 23068672 | tf_op jit(solution)/shard_map/dot_general | solution.py:103
  386.5 10.4 %fusion.17 = f32[1024,2048]{1,0:T(8,128)} fusion(bf16[1024,1024]{1,0:T(8,128)(2,1)S(1)} %get-tuple-element.89, bf16[2,2048,1024]{2,1,0:T(8,128)(2,1)} %all-gather.13.cloned.1.call-done), kind=kOutput, calls=%fused_computation.66 | convolution fusion | flops 4294967296 | bytes 14680064 | tf_op jit(solution)/shard_map/dot_general | solution.py:103
  397.0 9.1 %fusion.19 = f32[1024,2048]{1,0:T(8,128)} fusion(bf16[1024,1024]{1,0:T(8,128)(2,1)S(1)} %get-tuple-element.88, bf16[2,2048,1024]{2,1,0:T(8,128)(2,1)} %all-gather.15.cloned.1.call-done), kind=kOutput, calls=%fused_computation.68 | convolution fusion | flops 4294967296 | bytes 14680064 | tf_op jit(solution)/shard_map/dot_general | solution.py:103
  406.1 10.7 %multiply_convert_fusion.3 = (bf16[1024,1024]{1,0:T(8,128)(2,1)S(1)}, bf16[1024,1024]{1,0:T(8,128)(2,1)}, bf16[1024,1024]{1,0:T(8,128)(2,1)}) fusion(f32[1024,1024]{1,0:T(8,128)} %fusion.23, f32[1024,1024]{1,0:T(8,128)} %fusion.24, bf16[1024,2048]{1,0:T(8,128)(2,1)S(1)} %bitcast.455, bf16[2,1024,2048]{2,1,0:T(8,128)(2,1)S(1)} %bitcast.532), kind=kOutput, calls=%fused_computation.47 | convolution fusion | flops 4310695936 | bytes 23068672 | tf_op jit(solution)/shard_map/dot_general | solution.py:103
  416.8 9.1 %fusion.22 = f32[1024,2048]{1,0:T(8,128)} fusion(bf16[1024,1024]{1,0:T(8,128)(2,1)} %get-tuple-element.86, bf16[2,2048,1024]{2,1,0:T(8,128)(2,1)S(1)} %bitcast.534), kind=kOutput, calls=%fused_computation.71 | convolution fusion | flops 4294967296 | bytes 14680064 | tf_op jit(solution)/shard_map/dot_general | solution.py:103
  425.9 13.3 %add_convert_fusion = bf16[1024,2048]{1,0:T(8,128)(2,1)} fusion(f32[1024,2048]{1,0:T(8,128)} %fusion.22, f32[1024,2048]{1,0:T(8,128)} %fusion.17, f32[1024,2048]{1,0:T(8,128)} %fusion.19, bf16[1024,1024]{1,0:T(8,128)(2,1)S(1)} %get-tuple-element.85, bf16[2,2048,1024]{2,1,0:T(8,128)(2,1)} %all-gather.15.cloned.1.call-done), kind=kOutput, calls=%fused_computation.28 | convolution fusion | flops 4303355904 | bytes 35651584 | tf_op jit(solution)/shard_map/dot_general | solution.py:103
  451.9 9.0 %collective-permute-done.41 = bf16[128,2048]{1,0:T(8,128)(2,1)S(1)} collective-permute-done((bf16[128,2048]{1,0:T(8,128)(2,1)S(1)}, bf16[128,2048]{1,0:T(8,128)(2,1)S(1)}, u32[]{:S(2)}, u32[]{:S(2)}) %collective-permute-start.41) | collective-permute-done | bytes 524320 | tf_op jit(solution)/shard_map/ppermute | solution.py:86
  463.7 7.5 convolution_convert_fusion.1
  474.7 12.6 %fusion.2 = (f32[1024]{0:T(1024)S(1)}, f32[1024]{0:T(1024)S(1)}, bf16[1024,2048]{1,0:T(8,128)(2,1)}, bf16[1024,2048]{1,0:T(8,128)(2,1)}, bf16[1024,2048]{1,0:T(8,128)(2,1)}) fusion(bf16[8,128,2048]{2,1,0:T(8,128)(2,1)} %fusion.77, bf16[1024,2048]{1,0:T(8,128)(2,1)S(1)} %convolution_convert_fusion.1, f32[1024]{0:T(1024)S(1)} %bitcast.502, ...), kind=kOutput, calls=%fused_computation.6 | convolution fusion | flops 4328519680 | bytes 27279360 | tf_op jit(solution)/shard_map/dot_general | solution.py:103
  552.0 19.8 %psum.7 = f32[2,1024]{1,0:T(2,128)S(1)} all-reduce(f32[2,1024]{1,0:T(2,128)S(1)} %pad_maximum_fusion.17), channel_id=1, replica_groups=mesh['head'=8,'fsdp'=4] {'head'}, use_global_device_ids=true, to_apply=%region_23.24 | all-reduce | flops 2048 | bytes 16384 | tf_op jit(solution)/shard_map/psum | solution.py:284
  580.0 7.6 convert_bitcast_fusion.1
  600.3 7.6 convert_bitcast_fusion.3
  622.4 7.7 convert_bitcast_fusion.5
  672.4 9.8 %collective-permute-done.58 = bf16[128,2048]{1,0:T(8,128)(2,1)S(1)} collective-permute-done((bf16[128,2048]{1,0:T(8,128)(2,1)S(1)}, bf16[128,2048]{1,0:T(8,128)(2,1)S(1)}, u32[]{:S(2)}, u32[]{:S(2)}) %collective-permute-start.58) | collective-permute-done | bytes 524320 | tf_op jit(solution)/shard_map/ppermute | solution.py:56
  688.9 7.3 collective-permute-done.60
  697.6 13.4 %collective-permute-done.49 = bf16[128,2048]{1,0:T(8,128)(2,1)S(1)} collective-permute-done((bf16[128,2048]{1,0:T(8,128)(2,1)S(1)}, bf16[128,2048]{1,0:T(8,128)(2,1)S(1)}, u32[]{:S(2)}, u32[]{:S(2)}) %collective-permute-start.49) | collective-permute-done | bytes 524320 | tf_op jit(solution)/shard_map/ppermute | solution.py:86
  770.0 23.5 %collective-permute-done.31 = bf16[128,2048]{1,0:T(8,128)(2,1)S(1)} collective-permute-done((bf16[128,2048]{1,0:T(8,128)(2,1)S(1)}, bf16[128,2048]{1,0:T(8,128)(2,1)S(1)}, u32[]{:S(2)}, u32[]{:S(2)}) %collective-permute-start.31) | collective-permute-done | bytes 524320 | tf_op jit(solution)/shard_map/ppermute | solution.py:87
  811.0 27.8 %reduce-scatter.10.cloned.1.call-done = bf16[2,512,1024]{2,1,0:T(8,128)(2,1)} async-done(((bf16[2,2048,1024]{2,1,0:T(8,128)(2,1)}), bf16[2,512,1024]{2,1,0:T(8,128)(2,1)}) %reduce-scatter.10.cloned.1.call-update) | async-done | bytes 2097168 | tf_op jit(solution)/shard_map/reduce_scatter | solution.py:234
  842.9 30.4 %reduce-scatter.8.cloned.1.call-done = f32[64,2048]{1,0:T(8,128)} async-done(((f32[256,2048]{1,0:T(8,128)}), f32[64,2048]{1,0:T(8,128)}) %reduce-scatter.8.cloned.1.call-update) | async-done | bytes 524304 | tf_op jit(solution)/shard_map/reduce_scatter | solution.py:303
  (528 shorter events, 391.1 us)
Async XLA Ops:
  7.2 206.4 %all-gather.9.cloned.1.call-start = ((), (), s32[]{:S(2)}) async-start(), calls=%async_computation.10 | async-start | bytes 3932160 | tf_op jit(solution)/shard_map/all_gather | solution.py:150
  37.5 277.4 %all-gather.11.cloned.1.call-start = ((), (), s32[]{:S(2)}) async-start(), calls=%async_computation.11 | async-start | bytes 8650752 | tf_op jit(solution)/shard_map/all_gather | solution.py:153
  38.2 303.5 %all-gather.13.cloned.1.call-start = ((), (), s32[]{:S(2)}) async-start(), calls=%async_computation.12 | async-start | bytes 10485760 | tf_op jit(solution)/shard_map/all_gather | solution.py:154
  39.0 319.1 %all-gather.15.cloned.1.call-start = ((), (), s32[]{:S(2)}) async-start(), calls=%async_computation.13 | async-start | bytes 10485760 | tf_op jit(solution)/shard_map/all_gather | solution.py:155
  39.5 334.8 %all-gather.17.cloned.1.call-start = ((), (), s32[]{:S(2)}) async-start(), calls=%async_computation.14 | async-start | bytes 10485760 | tf_op jit(solution)/shard_map/all_gather | solution.py:156
  39.6 69.0 %collective-permute-start.16 = (s32[128,16]{0,1:T(8,128)S(1)}, s32[128,16]{0,1:T(8,128)S(1)}, u32[]{:S(2)}, u32[]{:S(2)}) collective-permute-start(s32[128,16]{0,1:T(8,128)S(1)} %pad_add_fusion), channel_id=1, source_target_pairs={{0,8},{8,16},{16,24},{24,28},{28,20},{20,12},{12,4},{4,0},{1,9},{9... | collective-permute-start | bytes 24584 | tf_op jit(solution)/shard_map/ppermute | solution.py:56
  40.8 67.9 %collective-permute-start.17 = (s32[128,16]{0,1:T(8,128)S(1)}, s32[128,16]{0,1:T(8,128)S(1)}, u32[]{:S(2)}, u32[]{:S(2)}) collective-permute-start(s32[128,16]{0,1:T(8,128)S(1)} %pad_add_fusion), channel_id=1, source_target_pairs={{8,0},{16,8},{24,16},{28,24},{20,28},{12,20},{4,12},{0,4},{9,1},{1... | collective-permute-start | bytes 24584 | tf_op jit(solution)/shard_map/ppermute | solution.py:57
  41.7 80.4 %collective-permute-start = (bf16[128,2048]{1,0:T(8,128)(2,1)S(1)}, bf16[128,2048]{1,0:T(8,128)(2,1)S(1)}, u32[]{:S(2)}, u32[]{:S(2)}) collective-permute-start(bf16[128,2048]{1,0:T(8,128)(2,1)S(1)} %bitcast.422), channel_id=1, source_target_pairs={{0,8},{8,16},{16,24},{24,28},{28,20},{20,12},{12,4},{4,0},{1,9},{9... | collective-permute-start | bytes 1572872 | tf_op jit(solution)/shard_map/ppermute | solution.py:56
  42.8 80.6 %collective-permute-start.1 = (bf16[128,2048]{1,0:T(8,128)(2,1)S(1)}, bf16[128,2048]{1,0:T(8,128)(2,1)S(1)}, u32[]{:S(2)}, u32[]{:S(2)}) collective-permute-start(bf16[128,2048]{1,0:T(8,128)(2,1)S(1)} %bitcast.423), channel_id=1, source_target_pairs={{8,0},{16,8},{24,16},{28,24},{20,28},{12,20},{4,12},{0,4},{9,1},{1... | collective-permute-start | bytes 1572872 | tf_op jit(solution)/shard_map/ppermute | solution.py:57
  43.7 82.2 %collective-permute-start.32 = (bf16[128,2048]{1,0:T(8,128)(2,1)S(1)}, bf16[128,2048]{1,0:T(8,128)(2,1)S(1)}, u32[]{:S(2)}, u32[]{:S(2)}) collective-permute-start(bf16[128,2048]{1,0:T(8,128)(2,1)S(1)} %bitcast.436), channel_id=1, source_target_pairs={{0,8},{8,16},{16,24},{24,28},{28,20},{20,12},{12,4},{4,0},{1,9},{9... | collective-permute-start | bytes 1572872 | tf_op jit(solution)/shard_map/ppermute | solution.py:56
  120.3 32.1 %collective-permute-start.33 = (bf16[128,2048]{1,0:T(8,128)(2,1)S(1)}, bf16[128,2048]{1,0:T(8,128)(2,1)}, u32[]{:S(2)}, u32[]{:S(2)}) collective-permute-start(bf16[128,2048]{1,0:T(8,128)(2,1)S(1)} %bitcast.437), channel_id=1, source_target_pairs={{8,0},{16,8},{24,16},{28,24},{20,28},{12,20},{4,12},{0,4},{9,1},{1... | collective-permute-start | bytes 1572872 | tf_op jit(solution)/shard_map/ppermute | solution.py:57
  122.2 32.2 %collective-permute-start.2 = (bf16[128,2048]{1,0:T(8,128)(2,1)S(1)}, bf16[128,2048]{1,0:T(8,128)(2,1)S(1)}, u32[]{:S(2)}, u32[]{:S(2)}) collective-permute-start(bf16[128,2048]{1,0:T(8,128)(2,1)S(1)} %collective-permute-done), channel_id=1, source_target_pairs={{0,8},{8,16},{16,24},{24,28},{28,20},{20,12},{12,4},{4,0},{1,9},{9... | collective-permute-start | bytes 1572872 | tf_op jit(solution)/shard_map/ppermute | solution.py:56
  123.4 41.0 %collective-permute-start.3 = (bf16[128,2048]{1,0:T(8,128)(2,1)S(1)}, bf16[128,2048]{1,0:T(8,128)(2,1)S(1)}, u32[]{:S(2)}, u32[]{:S(2)}) collective-permute-start(bf16[128,2048]{1,0:T(8,128)(2,1)S(1)} %collective-permute-done.1), channel_id=1, source_target_pairs={{8,0},{16,8},{24,16},{28,24},{20,28},{12,20},{4,12},{0,4},{9,1},{1... | collective-permute-start | bytes 1572872 | tf_op jit(solution)/shard_map/ppermute | solution.py:57
  125.9 38.7 %collective-permute-start.34 = (bf16[128,2048]{1,0:T(8,128)(2,1)S(1)}, bf16[128,2048]{1,0:T(8,128)(2,1)S(1)}, u32[]{:S(2)}, u32[]{:S(2)}) collective-permute-start(bf16[128,2048]{1,0:T(8,128)(2,1)S(1)} %collective-permute-done.32), channel_id=1, source_target_pairs={{0,8},{8,16},{16,24},{24,28},{28,20},{20,12},{12,4},{4,0},{1,9},{9... | collective-permute-start | bytes 1572872 | tf_op jit(solution)/shard_map/ppermute | solution.py:56
  152.4 23.3 %collective-permute-start.35 = (bf16[128,2048]{1,0:T(8,128)(2,1)}, bf16[128,2048]{1,0:T(8,128)(2,1)S(1)}, u32[]{:S(2)}, u32[]{:S(2)}) collective-permute-start(bf16[128,2048]{1,0:T(8,128)(2,1)} %collective-permute-done.33), channel_id=1, source_target_pairs={{8,0},{16,8},{24,16},{28,24},{20,28},{12,20},{4,12},{0,4},{9,1},{1... | collective-permute-start | bytes 1572872 | tf_op jit(solution)/shard_map/ppermute | solution.py:57
  154.3 23.2 %collective-permute-start.4 = (bf16[128,2048]{1,0:T(8,128)(2,1)S(1)}, bf16[128,2048]{1,0:T(8,128)(2,1)S(1)}, u32[]{:S(2)}, u32[]{:S(2)}) collective-permute-start(bf16[128,2048]{1,0:T(8,128)(2,1)S(1)} %collective-permute-done.2), channel_id=1, source_target_pairs={{0,8},{8,16},{16,24},{24,28},{28,20},{20,12},{12,4},{4,0},{1,9},{9... | collective-permute-start | bytes 1572872 | tf_op jit(solution)/shard_map/ppermute | solution.py:56
  164.5 22.5 %collective-permute-start.5 = (bf16[128,2048]{1,0:T(8,128)(2,1)S(1)}, bf16[128,2048]{1,0:T(8,128)(2,1)S(1)}, u32[]{:S(2)}, u32[]{:S(2)}) collective-permute-start(bf16[128,2048]{1,0:T(8,128)(2,1)S(1)} %collective-permute-done.3), channel_id=1, source_target_pairs={{8,0},{16,8},{24,16},{28,24},{20,28},{12,20},{4,12},{0,4},{9,1},{1... | collective-permute-start | bytes 1572872 | tf_op jit(solution)/shard_map/ppermute | solution.py:57
  164.6 22.5 %collective-permute-start.36 = (bf16[128,2048]{1,0:T(8,128)(2,1)S(1)}, bf16[128,2048]{1,0:T(8,128)(2,1)S(1)}, u32[]{:S(2)}, u32[]{:S(2)}) collective-permute-start(bf16[128,2048]{1,0:T(8,128)(2,1)S(1)} %collective-permute-done.34), channel_id=1, source_target_pairs={{0,8},{8,16},{16,24},{24,28},{28,20},{20,12},{12,4},{4,0},{1,9},{9... | collective-permute-start | bytes 1572872 | tf_op jit(solution)/shard_map/ppermute | solution.py:56
  177.6 24.1 %collective-permute-start.6 = (bf16[64,2048]{1,0:T(8,128)(2,1)S(1)}, bf16[64,2048]{1,0:T(8,128)(2,1)S(1)}, u32[]{:S(2)}, u32[]{:S(2)}) collective-permute-start(bf16[64,2048]{1,0:T(8,128)(2,1)S(1)} %slice.410), channel_id=1, source_target_pairs={{0,8},{8,16},{16,24},{24,28},{28,20},{20,12},{12,4},{4,0},{1,9},{9... | collective-permute-start | bytes 786440 | tf_op jit(solution)/shard_map/ppermute | solution.py:60
  188.6 95.7 %collective-permute-start.38 = (bf16[64,2048]{1,0:T(8,128)(2,1)}, bf16[64,2048]{1,0:T(8,128)(2,1)}, u32[]{:S(2)}, u32[]{:S(2)}) collective-permute-start(bf16[64,2048]{1,0:T(8,128)(2,1)} %slice.443), channel_id=1, source_target_pairs={{0,8},{8,16},{16,24},{24,28},{28,20},{20,12},{12,4},{4,0},{1,9},{9... | collective-permute-start | bytes 786440 | tf_op jit(solution)/shard_map/ppermute | solution.py:60
  199.7 84.6 %collective-permute-start.39 = (bf16[64,2048]{1,0:T(8,128)(2,1)}, bf16[64,2048]{1,0:T(8,128)(2,1)}, u32[]{:S(2)}, u32[]{:S(2)}) collective-permute-start(bf16[64,2048]{1,0:T(8,128)(2,1)} %slice.444), channel_id=1, source_target_pairs={{8,0},{16,8},{24,16},{28,24},{20,28},{12,20},{4,12},{0,4},{9,1},{1... | collective-permute-start | bytes 786440 | tf_op jit(solution)/shard_map/ppermute | solution.py:61
  523.5 239.0 %reduce-scatter.6.cloned.1.call-start = ((), (), s32[]{:S(2)}) async-start(), calls=%async_computation.15 | async-start | bytes 3932160 | tf_op jit(solution)/shard_map/reduce_scatter | solution.py:298
  579.5 223.3 %reduce-scatter.14.cloned.1.call-start = ((), (), s32[]{:S(2)}) async-start(), calls=%async_computation.19 | async-start | bytes 10485760 | tf_op jit(solution)/shard_map/reduce_scatter | solution.py:234
  600.2 206.7 %reduce-scatter.12.cloned.1.call-start = ((), (), s32[]{:S(2)}) async-start(), calls=%async_computation.18 | async-start | bytes 10485760 | tf_op jit(solution)/shard_map/reduce_scatter | solution.py:234
  620.5 218.2 %reduce-scatter.10.cloned.1.call-start = ((), (), s32[]{:S(2)}) async-start(), calls=%async_computation.17 | async-start | bytes 10485760 | tf_op jit(solution)/shard_map/reduce_scatter | solution.py:234
  642.6 230.6 %reduce-scatter.8.cloned.1.call-start = ((), (), s32[]{:S(2)}) async-start(), calls=%async_computation.16 | async-start | bytes 2621440 | tf_op jit(solution)/shard_map/reduce_scatter | solution.py:303
  654.6 83.7 %collective-permute-start.29 = (bf16[128,2048]{1,0:T(8,128)(2,1)S(1)}, bf16[128,2048]{1,0:T(8,128)(2,1)}, u32[]{:S(2)}, u32[]{:S(2)}) collective-permute-start(bf16[128,2048]{1,0:T(8,128)(2,1)S(1)} %pad_maximum_fusion.10), channel_id=1, source_target_pairs={{8,0},{16,8},{24,16},{28,24},{20,28},{12,20},{4,12},{0,4},{9,1},{1... | collective-permute-start | bytes 1572872 | tf_op jit(solution)/shard_map/ppermute | solution.py:87
  656.5 71.4 %collective-permute-start.25 = (bf16[128,2048]{1,0:T(8,128)(2,1)S(1)}, bf16[128,2048]{1,0:T(8,128)(2,1)S(1)}, u32[]{:S(2)}, u32[]{:S(2)}) collective-permute-start(bf16[128,2048]{1,0:T(8,128)(2,1)S(1)} %pad_maximum_fusion.9), channel_id=1, source_target_pairs={{0,8},{8,16},{16,24},{24,28},{28,20},{20,12},{12,4},{4,0},{1,9},{9... | collective-permute-start | bytes 1572872 | tf_op jit(solution)/shard_map/ppermute | solution.py:86
  688.7 34.3 %collective-permute-start.53 = (bf16[128,2048]{1,0:T(8,128)(2,1)S(1)}, bf16[128,2048]{1,0:T(8,128)(2,1)}, u32[]{:S(2)}, u32[]{:S(2)}) collective-permute-start(bf16[128,2048]{1,0:T(8,128)(2,1)S(1)} %pad_maximum_fusion.14), channel_id=1, source_target_pairs={{8,0},{16,8},{24,16},{28,24},{20,28},{12,20},{4,12},{0,4},{9,1},{1... | collective-permute-start | bytes 1572872 | tf_op jit(solution)/shard_map/ppermute | solution.py:87
  741.3 24.8 %collective-permute-start.30 = (bf16[128,2048]{1,0:T(8,128)(2,1)}, bf16[128,2048]{1,0:T(8,128)(2,1)}, u32[]{:S(2)}, u32[]{:S(2)}) collective-permute-start(bf16[128,2048]{1,0:T(8,128)(2,1)} %get-tuple-element.113), channel_id=1, source_target_pairs={{8,0},{16,8},{24,16},{28,24},{20,28},{12,20},{4,12},{0,4},{9,1},{1... | collective-permute-start | bytes 1572872 | tf_op jit(solution)/shard_map/ppermute | solution.py:87
  762.5 36.8 %all-to-all-start.3 = ((bf16[8,64,768]{2,1,0:T(8,128)(2,1)}), bf16[8,64,768]{2,1,0:T(8,128)(2,1)S(1)}, u32[]{:S(2)}, u32[]{:S(2)}) async-start(bf16[8,64,768]{2,1,0:T(8,128)(2,1)} %reduce-scatter.6.cloned.1.call-done), calls=%async_computation.4 | async-start | bytes 1572864 | tf_op jit(solution)/shard_map/all_to_all | solution.py:299
  767.4 26.1 %collective-permute-start.31 = (bf16[128,2048]{1,0:T(8,128)(2,1)S(1)}, bf16[128,2048]{1,0:T(8,128)(2,1)S(1)}, u32[]{:S(2)}, u32[]{:S(2)}) collective-permute-start(bf16[128,2048]{1,0:T(8,128)(2,1)S(1)} %fusion.60), channel_id=1, source_target_pairs={{8,0},{16,8},{24,16},{28,24},{20,28},{12,20},{4,12},{0,4},{9,1},{1... | collective-permute-start | bytes 1572872 | tf_op jit(solution)/shard_map/ppermute | solution.py:87
  (141 other events, 2050.1 us)
Sparse Core Ops, SparseCore 0:
  37.6 28.0 all-gather.8
  68.6 92.0 all-gather.10
  162.2 65.0 all-gather.12
  228.8 58.2 all-gather.14
  288.5 58.2 all-gather.16
  579.6 34.0 reduce-scatter.5
  616.4 71.6 reduce-scatter.13
  690.8 73.4 reduce-scatter.11
  767.0 71.7 reduce-scatter.9
  841.7 31.4 reduce-scatter.7
